TPU v7x, 32 devices: a whole 2x2x4 slice. The times are simulated.
32 devices in a mesh: space: 4 (over z), vel: 8 (over y, x, core).
Axes of the slice: x: 2, y: 2, z: 4, core: 2. Of those that a mesh axis runs over, the one named last changes fastest.
Arguments:
- dist: float32 [64, 16, 16, 2048], P('space', None, None, 'vel'), may hold values from 0.05 to 2
- relax_rate: float32 [64, 16, 16], P('space'), may hold values from 0.2 to 0.9
- kinetic_cells: int32 [2, 16384], P(None, 'space'), may hold values from 0 to 4095, as said below
- kinetic_count: int32 [2, 4], replicated, may hold values from 1 to 4096, 8192 in all within a row
- map_a: bfloat16 [2048, 768], replicated, may hold values from -0.125 to 0.125
- map_b: bfloat16 [2048, 768], replicated, may hold values from -0.125 to 0.125
- map_c: bfloat16 [768, 2048], replicated, may hold values from -0.21875 to 0.21875
Outputs:
- dist_out: float32 [64, 16, 16, 2048], P('space', None, None, 'vel')
Inputs may be any that keep to these rules, and one draw needn't show every extreme that they name: `kinetic_cells`: for each step, the 4096 entries of a slab's block are a permutation of that slab's local cell numbers. `kinetic_count`: each step's counts sum to 8192, and one slab is kinetic in all its cells.
All inputs are finite; a program needn't handle non-finite values.
Results may differ from a plain program's by a relative error of at most 0.0034.
Values may be sent and summed in bfloat16 or wider, within the bound.
A program may use at most 128 MiB of HBM per device.

v0:
```python
import functools
import math

import jax
import jax.numpy as jnp
import numpy as np
from jax import lax
from jax.experimental import pallas as pl
from jax.experimental.pallas import tpu as pltpu
from jax.sharding import PartitionSpec as P

GX = 16
GY = 16
GZ = 8
STEPS = 2
COURANT = 0.1
SPACING = 0.5
COLLIDE = 0.5
LANES = 128
CHUNKS = 4
LAG = 1
MESH = pl.DeviceIdType.MESH


def tables():
    k = np.arange(GX * GY * GZ)
    vx = ((k // (GY * GZ)) - 0.5 * (GX - 1)) * SPACING
    vy = (((k // GZ) % GY) - 0.5 * (GY - 1)) * SPACING
    vz = ((k % GZ) - 0.5 * (GZ - 1)) * SPACING
    s = vx * vx + vy * vy + vz * vz
    w = np.exp(-0.5 * s)
    w = w / w.sum()
    m2, m4 = (w * s).sum(), (w * s * s).sum()
    kappa = m4 - m2 * m2
    per_e = w * (s - m2) / kappa
    rows = np.stack([
        w - m2 * per_e,
        w * vx / (w * vx * vx).sum(),
        w * vy / (w * vy * vy).sum(),
        w * vz / (w * vz * vz).sum(),
        per_e,
        per_e,
    ])
    s_hi = np.asarray(np.asarray(s, np.float32).astype(jnp.bfloat16), np.float64)
    cols = np.stack([np.ones_like(vx), vx, vy, vz, s_hi, s - s_hi], axis=1)
    g_hi = np.asarray(np.asarray(rows, np.float32).astype(jnp.bfloat16), np.float64)
    g_lo = rows - g_hi
    basis = np.zeros((24, k.size))
    back = np.zeros((24, k.size))
    for at, part in ((0, g_hi), (8, g_hi), (16, g_lo)):
        basis[at:at + 6] = cols.T
        back[at:at + 6] = part
    return basis.astype(np.float32), back.astype(np.float32)


def limited(a, b):
    return jnp.minimum(jnp.maximum(a, jnp.minimum(b, 0.0)), jnp.maximum(b, 0.0))


def merged(code_row, moved, payload, own_back):
    code = jnp.broadcast_to(code_row, (LANES, LANES)).T
    equilibrium = jnp.dot(payload[:, :LANES], own_back, preferred_element_type=jnp.float32)
    out = []
    for t in range(moved.shape[1] // LANES):
        cols = slice(t * LANES, (t + 1) * LANES)
        old = moved[:, cols]
        fluid = old + code * (equilibrium[:, cols] - old)
        out.append(jnp.where(code < 0.0, old - code * payload[:, cols].astype(jnp.float32), fluid))
    return jnp.concatenate(out, axis=1)


def kernel(dims, counts, kin_cells, relax, basis_rows, back, dist, a_hbm, b_hbm, c_hbm,
           moved_out, ret_out, codes,
           cur, moved, cprev, halo, sendbuf, recv, res, ret, map_a, map_b, map_c, basis, spread,
           load_sem, const_sem, local_sem, out_sem, halo_send, halo_recv, row_send, row_recv, res_send, res_recv):
    nx, ny, nz, width, groups, slabs = dims
    plane = ny * nz
    cells = nx * plane
    chunk = cells // CHUNKS
    rows = chunk // groups
    planes = nx // CHUNKS
    tiles = width // LANES
    me = lax.axis_index("vel")
    slab = lax.axis_index("space")
    first_x = (me * width) // (GY * GZ)
    bit = first_x // (GX // 2)
    sign = 2 * bit - 1
    ahead = lax.rem(slab + sign + slabs, slabs)
    behind = lax.rem(slab - sign + slabs, slabs)

    pieces = [0, CHUNKS - 1] + list(range(1, CHUNKS - 1))
    loads = {}
    for c in pieces:
        loads[c] = pltpu.make_async_copy(
            dist.at[pl.ds(c * chunk, chunk)], cur.at[pl.ds(2 * plane + c * chunk, chunk)], load_sem.at[c])
        loads[c].start()
    consts = []
    for n, (src, dst) in enumerate(((a_hbm, map_a), (b_hbm, map_b), (c_hbm, map_c))):
        consts.append(pltpu.make_async_copy(src, dst, const_sem.at[n]))
        consts[-1].start()

    barrier = pltpu.get_barrier_semaphore()
    for p in range(1, groups):
        pl.semaphore_signal(barrier, inc=1, device_id={"vel": lax.rem(me + p, groups)}, device_id_type=MESH)
    pl.semaphore_signal(barrier, inc=1, device_id={"space": ahead}, device_id_type=MESH)
    pl.semaphore_signal(barrier, inc=1, device_id={"space": behind}, device_id_type=MESH)
    pl.semaphore_wait(barrier, groups + 1)

    lane = lax.broadcasted_iota(jnp.int32, (1, LANES), 1)
    vy = (((lane // GZ) % GY).astype(jnp.float32) - 0.5 * (GY - 1)) * SPACING
    vz = ((lane % GZ).astype(jnp.float32) - 0.5 * (GZ - 1)) * SPACING
    block = (nz, LANES)
    pos_y = jnp.broadcast_to(vy > 0.0, block)
    pos_z = jnp.broadcast_to(vz > 0.0, block)
    half_y = jnp.broadcast_to(jnp.where(vy > 0.0, 0.5, -0.5), block)
    half_z = jnp.broadcast_to(jnp.where(vz > 0.0, 0.5, -0.5), block)
    rate_y = jnp.broadcast_to(COURANT * jnp.abs(vy), block)
    rate_z = jnp.broadcast_to(COURANT * jnp.abs(vz), block)

    def pick(positive, negative):
        return bit * positive + (1 - bit) * negative

    def at(index, y):
        return pl.ds(pl.multiple_of(index * plane + y * nz, nz), nz)

    def x_state(index, y, cols):
        mid = cur[at(index, y), cols]
        slope = limited(mid - cur[at(index - sign, y), cols], cur[at(index + sign, y), cols] - mid)
        return mid + 0.5 * slope

    def transport(c):
        start = pick(2 + c * planes, 2 + (c + 1) * planes - 1)

        @pl.loop(0, ny)
        def _(y):
            for t in range(tiles):
                cols = pl.ds(t * LANES, LANES)
                cprev[pl.ds(pl.multiple_of(y * nz, nz), nz), cols] = x_state(start - sign, y, cols)

        @pl.loop(0, planes)
        def _(j):
            index = start + sign * j
            @pl.loop(0, tiles)
            def _(t):
                cols = pl.ds(pl.multiple_of(t * LANES, LANES), LANES)
                vx = (((me * width + t * LANES) // (GY * GZ)).astype(jnp.float32) - 0.5 * (GX - 1)) * SPACING
                rate_x = COURANT * jnp.abs(vx)

                def value(y):
                    return cur[at(index, y % ny), cols]

                def y_state(mid, before, after):
                    return mid + half_y * limited(before, after)

                f = {y: value(y) for y in range(-2, 2)}
                d = {y: f[y + 1] - f[y] for y in (-2, -1, 0)}
                cy = {y: y_state(f[y], d[y - 1], d[y]) for y in (-1, 0)}
                for y in range(ny):
                    f[y + 2] = value(y + 2)
                    d[y + 1] = f[y + 2] - f[y + 1]
                    cy[y + 1] = y_state(f[y + 1], d[y], d[y + 1])
                    mid = f[y]
                    total = rate_y * (cy[y] - jnp.where(pos_y, cy[y - 1], cy[y + 1]))
                    dz = pltpu.roll(mid, nz - 1, 0) - mid
                    cz = mid + half_z * limited(pltpu.roll(dz, 1, 0), dz)
                    total += rate_z * (cz - jnp.where(pos_z, pltpu.roll(cz, 1, 0), pltpu.roll(cz, nz - 1, 0)))
                    cx = x_state(index, y, cols)
                    here = pl.ds(y * nz, nz)
                    total += rate_x * (cx - cprev[here, cols])
                    cprev[here, cols] = cx
                    result = mid - total
                    moved[at(index - 2, y), cols] = result
                    sendbuf[at(index - 2, y), cols] = result.astype(jnp.bfloat16)

    def prepare():
        @pl.loop(0, basis.shape[0] // LANES)
        def _(n):
            here = pl.ds(pl.multiple_of(n * LANES, LANES), LANES)
            part = basis_rows[:, here]
            whole = jnp.concatenate([part, jnp.zeros((LANES - part.shape[0], LANES), jnp.float32)], axis=0)
            basis[here] = whole.T.astype(jnp.bfloat16)

        groups_of = cells // LANES
        span = 4 * LANES
        for step in range(STEPS):
            count = counts[step, slab]
            flags = jnp.zeros((groups_of, LANES), jnp.float32)
            for n in range(cells // span):
                which = kin_cells[step:step + 1, n * span:(n + 1) * span]
                live = n * span + lax.broadcasted_iota(jnp.int32, (1, span), 1) < count
                quotient = jnp.where(live, lax.div(which, LANES), -1)
                hot_high = lax.broadcasted_iota(jnp.int32, (groups_of, span), 0) == quotient
                hot_low = lax.broadcasted_iota(jnp.int32, (LANES, span), 0) == lax.rem(which, LANES)
                flags += lax.dot_general(
                    jnp.where(hot_high, 1.0, 0.0).astype(jnp.bfloat16), jnp.where(hot_low, 1.0, 0.0).astype(jnp.bfloat16),
                    (((1,), (1,)), ((), ())), preferred_element_type=jnp.float32)
            codes[step] = jnp.where(flags > 0.5, -COLLIDE, relax[...])

    def row_copies(c):
        out = []
        for p in range(1, groups):
            peer = lax.rem(me + p, groups)
            out.append(pltpu.make_async_remote_copy(
                src_ref=sendbuf.at[pl.ds(pl.multiple_of(c * chunk + peer * rows, rows), rows)],
                dst_ref=recv.at[me, pl.ds(c * rows, rows)],
                send_sem=row_send.at[c, p], recv_sem=row_recv.at[c, p],
                device_id={"vel": peer}, device_id_type=MESH))
        return out

    def row_local(c):
        return pltpu.make_async_copy(
            sendbuf.at[pl.ds(pl.multiple_of(c * chunk + me * rows, rows), rows)],
            recv.at[me, pl.ds(c * rows, rows)], local_sem.at[0, c])

    def res_copies(c):
        out = []
        for p in range(1, groups):
            peer = lax.rem(me + p, groups)
            out.append(pltpu.make_async_remote_copy(
                src_ref=res.at[peer, pl.ds(c * rows, rows)],
                dst_ref=ret.at[pl.ds(pl.multiple_of(c * chunk + me * rows, rows), rows)],
                send_sem=res_send.at[c, p], recv_sem=res_recv.at[c, p],
                device_id={"vel": peer}, device_id_type=MESH))
        return out

    def res_local(c):
        return pltpu.make_async_copy(
            res.at[me, pl.ds(c * rows, rows)],
            ret.at[pl.ds(pl.multiple_of(c * chunk + me * rows, rows), rows)], local_sem.at[1, c])

    def collide(step, c):
        here = pl.ds(c * rows, rows)
        first = second = mom = None
        for s in range(groups):
            part = recv[s, here]
            cols = pl.ds(s * width, width)
            terms = [jnp.dot(part, m[cols], preferred_element_type=jnp.float32) for m in (map_a, map_b, basis)]
            first, second, mom = terms if s == 0 else [old + new for old, new in zip((first, second, mom), terms)]
        hidden = (first * second).astype(jnp.bfloat16)
        high = mom.astype(jnp.bfloat16).astype(jnp.float32)
        is_low = (lax.broadcasted_iota(jnp.int32, mom.shape, 1) // 8) == 1
        split = jnp.where(is_low, mom - high, high)
        begin = c * chunk + me * rows
        spread[...] = jnp.broadcast_to(codes[step, pl.ds(begin // LANES, 1)], (LANES, LANES)).T
        kin = spread[pl.ds(pl.multiple_of(lax.rem(begin, LANES), math.gcd(rows, LANES)), rows)] < 0.0
        for s in range(groups):
            cols = pl.ds(s * width, width)
            out = jnp.dot(hidden, map_c[:, cols], preferred_element_type=jnp.float32)
            res[s, here, :LANES] = jnp.where(kin, out[:, :LANES], split).astype(jnp.bfloat16)
            if tiles > 1:
                res[s, here, LANES:] = out[:, LANES:].astype(jnp.bfloat16)

    def update(step, c):
        own_back = back[...]

        @pl.loop(0, chunk // LANES)
        def _(n):
            base = pl.multiple_of(c * chunk + n * LANES, LANES)
            here = pl.ds(base, LANES)
            cur[pl.ds(2 * plane + base, LANES)] = merged(
                codes[step, pl.ds(c * (chunk // LANES) + n, 1)], moved[here], ret[here], own_back)

    def halo_copies(step):
        two, one = 2 * plane, plane
        ahead_src = pick(nx * plane, 2 * plane)
        behind_src = pick(2 * plane, (nx + 1) * plane)
        return [
            pltpu.make_async_remote_copy(
                src_ref=cur.at[pl.ds(pl.multiple_of(ahead_src, plane), two)], dst_ref=halo.at[step, pl.ds(0, two)],
                send_sem=halo_send.at[0], recv_sem=halo_recv.at[step, 0],
                device_id={"space": ahead}, device_id_type=MESH),
            pltpu.make_async_remote_copy(
                src_ref=cur.at[pl.ds(pl.multiple_of(behind_src, plane), one)], dst_ref=halo.at[step, pl.ds(two, one)],
                send_sem=halo_send.at[1], recv_sem=halo_recv.at[step, 1],
                device_id={"space": behind}, device_id_type=MESH),
        ]

    def halo_place(step):
        two, one = 2 * plane, plane
        up_dst = pick(0, (nx + 2) * plane)
        down_dst = pick((nx + 2) * plane, plane)
        return [
            pltpu.make_async_copy(halo.at[step, pl.ds(0, two)], cur.at[pl.ds(pl.multiple_of(up_dst, plane), two)],
                                  local_sem.at[2, 0]),
            pltpu.make_async_copy(halo.at[step, pl.ds(two, one)], cur.at[pl.ds(pl.multiple_of(down_dst, plane), one)],
                                  local_sem.at[2, 1]),
        ]

    outs = []
    sent, back_sent = {}, {}
    waiting = set()

    def finish(step, c):
        for copy in back_sent[c]:
            copy.wait()
        update(step, c)
        waiting.discard(c)

    def send_rows(step, c):
        sent[c] = row_copies(c)
        for copy in sent[c]:
            copy.start()
        own_copy = row_local(c)
        own_copy.start()
        sent[c].append(own_copy)
        if step == STEPS - 1:
            outs.append(pltpu.make_async_copy(
                moved.at[pl.ds(c * chunk, chunk)], moved_out.at[pl.ds(c * chunk, chunk)], out_sem.at[0, c]))
            outs[-1].start()

    def collide_send(step, c):
        for copy in sent[c]:
            copy.wait()
        collide(step, c)
        back_sent[c] = res_copies(c)
        for copy in back_sent[c]:
            copy.start()
        own_copy = res_local(c)
        own_copy.start()
        back_sent[c].append(own_copy)

    edges = [0, CHUNKS - 1]
    order = list(range(1, CHUNKS - 1)) + edges
    later = list(range(2, CHUNKS - 2)) + [1, CHUNKS - 2] + edges
    for step in range(STEPS):
        if step == 0:
            for c in edges:
                loads[c].wait()
            halos = halo_copies(step)
            for copy in halos:
                copy.start()
            loaded = set(edges)
        else:
            halos = None
            order = later
        queue = []
        for n, c in enumerate(order):
            near = [k for k in (c - 1, c, c + 1) if 0 <= k < CHUNKS]
            if step == 0:
                for k in near:
                    if k not in loaded:
                        loads[k].wait()
                        loaded.add(k)
            else:
                if n == max(CHUNKS - 4, 1):
                    near = sorted(waiting)
                for k in near:
                    if k in waiting:
                        finish(step - 1, k)
                if halos is None and not waiting.intersection(edges):
                    halos = halo_copies(step)
                    for copy in halos:
                        copy.start()
            if n == CHUNKS - 2:
                for copy in halos:
                    copy.wait()
                places = halo_place(step)
                for copy in places:
                    copy.start()
                for copy in places:
                    copy.wait()
            transport(c)
            send_rows(step, c)
            if step == 0 and n == 0:
                prepare()
                for copy in consts:
                    copy.wait()
            queue.append(c)
            if len(queue) > LAG:
                collide_send(step, queue.pop(0))
        while queue:
            collide_send(step, queue.pop(0))
        waiting = set(order)
    for c in order:
        for copy in back_sent[c]:
            copy.wait()
        outs.append(pltpu.make_async_copy(
            ret.at[pl.ds(c * chunk, chunk)], ret_out.at[pl.ds(c * chunk, chunk)], out_sem.at[1, c]))
        outs[-1].start()
    for copy in outs:
        copy.wait()


def final_kernel(codes, moved_ref, ret_ref, back_ref, out_ref):
    at = pl.program_id(0) * (out_ref.shape[0] // LANES)
    for n in range(out_ref.shape[0] // LANES):
        here = pl.ds(n * LANES, LANES)
        out_ref[here] = merged(codes[STEPS - 1, pl.ds(at + n, 1)], moved_ref[here], ret_ref[here], back_ref[...])


def body(dist, relax_rate, kinetic_cells, kinetic_count, map_a, map_b, map_c):
    nx, ny, nz, width = dist.shape
    groups = lax.axis_size("vel")
    slabs = lax.axis_size("space")
    cells = nx * ny * nz
    chunk = cells // CHUNKS
    rows = chunk // groups
    plane = ny * nz
    basis, back = tables()
    back = lax.dynamic_slice_in_dim(jnp.asarray(back), lax.axis_index("vel") * width, width, 1)
    back = jnp.pad(back, ((0, LANES - back.shape[0]), (0, 0))).astype(jnp.bfloat16)

    any_space = pl.BlockSpec(memory_space=pl.ANY)
    f32, bf16 = jnp.float32, jnp.bfloat16
    dims = (nx, ny, nz, width, groups, slabs)
    vmem = pl.BlockSpec(memory_space=pltpu.VMEM)
    moved, ret, codes = pl.pallas_call(
        functools.partial(kernel, dims),
        out_shape=(jax.ShapeDtypeStruct((cells, width), f32), jax.ShapeDtypeStruct((cells, width), bf16),
                   jax.ShapeDtypeStruct((STEPS, cells // LANES, LANES), f32)),
        in_specs=[pl.BlockSpec(memory_space=pltpu.SMEM)] + [vmem] * 4 + [any_space] * 4,
        out_specs=(any_space, any_space, vmem),
        scratch_shapes=[
            pltpu.VMEM(((nx + 4) * plane, width), f32),
            pltpu.VMEM((cells, width), f32),
            pltpu.VMEM((plane, width), f32),
            pltpu.VMEM((STEPS, 3 * plane, width), f32),
            pltpu.VMEM((cells, width), bf16),
            pltpu.VMEM((groups, CHUNKS * rows, width), bf16),
            pltpu.VMEM((groups, CHUNKS * rows, width), bf16),
            pltpu.VMEM((cells, width), bf16),
            pltpu.VMEM(map_a.shape, bf16),
            pltpu.VMEM(map_b.shape, bf16),
            pltpu.VMEM(map_c.shape, bf16),
            pltpu.VMEM((map_a.shape[0], LANES), bf16),
            pltpu.VMEM((LANES, LANES), f32),
            pltpu.SemaphoreType.DMA((CHUNKS,)),
            pltpu.SemaphoreType.DMA((3,)),
            pltpu.SemaphoreType.DMA((3, CHUNKS)),
            pltpu.SemaphoreType.DMA((2, CHUNKS)),
            pltpu.SemaphoreType.DMA((2,)),
            pltpu.SemaphoreType.DMA((STEPS, 2)),
            pltpu.SemaphoreType.DMA((CHUNKS, groups)),
            pltpu.SemaphoreType.DMA((CHUNKS, groups)),
            pltpu.SemaphoreType.DMA((CHUNKS, groups)),
            pltpu.SemaphoreType.DMA((CHUNKS, groups)),
        ],
        compiler_params=pltpu.CompilerParams(
            collective_id=0, has_side_effects=True, vmem_limit_bytes=67043328),
    )(kinetic_count, kinetic_cells, relax_rate.reshape(cells // LANES, LANES), jnp.asarray(basis), back,
      dist.reshape(cells, width), map_a, map_b, map_c)

    size = cells // 8
    out = pl.pallas_call(
        final_kernel,
        grid=(8,),
        out_shape=jax.ShapeDtypeStruct((cells, width), f32),
        in_specs=[
            pl.BlockSpec((STEPS, cells // LANES, LANES), lambda i: (0, 0, 0)),
            pl.BlockSpec((size, width), lambda i: (i, 0)),
            pl.BlockSpec((size, width), lambda i: (i, 0)),
            pl.BlockSpec((LANES, width), lambda i: (0, 0)),
        ],
        out_specs=pl.BlockSpec((size, width), lambda i: (i, 0)),
    )(codes, moved, ret, back)
    return out.reshape(dist.shape)


def solution(mesh):
    return jax.shard_map(
        body,
        mesh=mesh,
        in_specs=(
            P("space", None, None, "vel"),
            P("space", None, None),
            P(None, "space"),
            P(),
            P(),
            P(),
            P(),
        ),
        out_specs=P("space", None, None, "vel"),
        check_vma=False,
    )
```

profile of v0, /device:TPU:1, one launch (start us, length us, event | category | flops | bytes accessed | tf_op | source)
XLA Modules:
  0.0 124.6 jit_solution(8659194713108708557)
XLA Ops:
  0.0 0.7 dynamic-slice_convert_fusion
  0.7 1.6 %reshape.9.relax = f32[32,128]{1,0:T(8,128)} reshape(f32[16,16,16]{2,1,0:T(8,128)} %param.10) | data formatting | bytes 32768 | tf_op jit(solution)/shard_map/reshape | solution.py:440
  2.3 0.6 pad.5.back.back_ref
  2.9 113.9 %shard_map.91 = (f32[4096,256]{1,0:T(8,128)}, bf16[4096,256]{1,0:T(8,128)(2,1)}, f32[2,32,128]{2,1,0:T(8,128)}) custom-call(s32[2,4]{1,0:T(2,128)} %counts.1, s32[2,4096]{1,0:T(2,128)} %kin_cells.1, f32[32,128]{1,0:T(8,128)} %reshape.9.relax, f32[24,2048]{1,0:T(8,128)} %constant.18.clone.basis_rows, bf16[128,256]{1,0:T(8,128)(2,1)} %pad.5.back.back_ref, ...), custom_call_target="tpu_custom_call" | custom-call | tf_op jit(solution)/shard_map/pallas_call | solution.py:407
  116.9 7.8 %shard_map.92 = f32[4096,256]{1,0:T(8,128)} custom-call(f32[2,32,128]{2,1,0:T(8,128)} %get-tuple-element.8.codes, f32[4096,256]{1,0:T(8,128)} %get-tuple-element.9.moved_ref, bf16[4096,256]{1,0:T(8,128)(2,1)} %get-tuple-element.10.ret_ref, bf16[128,256]{1,0:T(8,128)(2,1)} %pad.5.back.back_ref), custom_call_target="tpu_custom_call" | custom-call | tf_op jit(solution)/shard_map/pallas_call | solution.py:444
where the time goes:
time: 125 us
  Pallas kernels  122 us (98%)
  local copies, waits for them, and re-layouts  2.94 us (2%)
    pallas_call x1, Pallas kernels, body(): pl.pallas_call(functools.partial(kernel, dims), out_shape=(jax.ShapeDtype...  114 us
    pallas_call x1, Pallas kernels, body(): pl.pallas_call(final_kernel, grid=(8,), out_shape=jax.ShapeDtypeStruct((c...  7.78 us

commit v1 on v0

v1 whole, which is shorter than its diff:
```python
import functools

import jax
import jax.numpy as jnp
import numpy as np
from jax import lax
from jax.experimental import pallas as pl
from jax.experimental.pallas import tpu as pltpu
from jax.sharding import PartitionSpec as P

GX = 16
GY = 16
GZ = 8
STEPS = 2
COURANT = 0.1
SPACING = 0.5
COLLIDE = 0.5
LANES = 128
TILE = 256
HALVES = 2
MESH = pl.DeviceIdType.MESH


def tables():
    k = np.arange(GX * GY * GZ)
    vx = ((k // (GY * GZ)) - 0.5 * (GX - 1)) * SPACING
    vy = (((k // GZ) % GY) - 0.5 * (GY - 1)) * SPACING
    vz = ((k % GZ) - 0.5 * (GZ - 1)) * SPACING
    s = vx * vx + vy * vy + vz * vz
    w = np.exp(-0.5 * s)
    w = w / w.sum()
    m2, m4 = (w * s).sum(), (w * s * s).sum()
    kappa = m4 - m2 * m2
    per_e = w * (s - m2) / kappa
    rows = np.stack([
        w - m2 * per_e,
        w * vx / (w * vx * vx).sum(),
        w * vy / (w * vy * vy).sum(),
        w * vz / (w * vz * vz).sum(),
        per_e,
        per_e,
    ])
    s_hi = np.asarray(np.asarray(s, np.float32).astype(jnp.bfloat16), np.float64)
    cols = np.stack([np.ones_like(vx), vx, vy, vz, s_hi, s - s_hi], axis=1)
    g_hi = np.asarray(np.asarray(rows, np.float32).astype(jnp.bfloat16), np.float64)
    g_lo = rows - g_hi
    basis = np.zeros((k.size, LANES))
    back = np.zeros((LANES, k.size))
    for at, part in ((0, g_hi), (8, g_hi), (16, g_lo)):
        basis[:, at:at + 6] = cols
        back[at:at + 6] = part
    return basis.astype(np.float32).astype(jnp.bfloat16), back.astype(np.float32).astype(jnp.bfloat16)


def limited(a, b):
    return jnp.minimum(jnp.maximum(a, jnp.minimum(b, 0.0)), jnp.maximum(b, 0.0))


def state(up, mid, down):
    return mid + 0.5 * limited(mid - up, down - mid)


def kernel(dims, counts, kin_cells, relax, dist, a_hbm, b_hbm, c_hbm, basis_hbm, back_hbm,
           ret_out,
           cur, cprev, sendbuf, zsend, zrecv, recv, fown, fsend, halo, mv, outbuf,
           map_a, map_b, map_c, basis, hid, coef,
           load_sem, const_sem, local_sem, z_send, z_recv, row_send, row_recv, halo_send, halo_recv, res_send, res_recv):
    nx, ny, nz, width, groups, slabs = dims
    plane = ny * nz
    cells = nx * plane
    nv = groups * width
    rank = map_a.shape[1]
    ppd = nx // groups
    hy = ny // HALVES
    half = hy * nz
    block_rows = ppd * half
    tiles = width // LANES
    nchips = groups // 2
    ncol = groups // 4
    me = lax.axis_index("vel")
    slab = lax.axis_index("space")
    first_x = lax.div(me * width, GY * GZ)
    bit = lax.div(first_x, GX // 2)
    sign = 2 * bit - 1
    ahead = lax.rem(slab + sign + slabs, slabs)
    behind = lax.rem(slab - sign + slabs, slabs)

    def vel_of(s, p):
        q = lax.rem(lax.div(p, 2) + nchips * slabs - s, nchips)
        y = lax.div(q, ncol)
        x = lax.rem(q, ncol)
        return (y * ncol + x + y * (ncol - 1 - 2 * x)) * 2 + lax.rem(p, 2)

    def chain_of(s, v):
        chip = lax.div(v, 2)
        y = lax.div(chip, ncol)
        x = lax.rem(chip, ncol)
        q = y * ncol + x + y * (ncol - 1 - 2 * x)
        return 2 * lax.rem(q + s, nchips) + lax.rem(v, 2)

    mine = chain_of(slab, me)

    def along(r):
        at = mine + r + groups
        s = lax.rem(slab + lax.div(at, groups) - 1 + slabs, slabs)
        return {"space": s, "vel": vel_of(s, lax.rem(at, groups))}

    pieces = 4
    loads = []
    for c in range(pieces):
        size = cells // pieces
        loads.append(pltpu.make_async_copy(
            dist.at[pl.ds(c * size, size)], cur.at[pl.ds(2 * plane + c * size, size)], load_sem.at[c]))
        loads[-1].start()
    consts = []
    for n, (src, dst) in enumerate(((a_hbm, map_a), (b_hbm, map_b), (c_hbm, map_c.at[pl.ds(0, rank)]),
                                    (back_hbm, map_c.at[pl.ds(rank, LANES)]), (basis_hbm, basis))):
        consts.append(pltpu.make_async_copy(src, dst, const_sem.at[n]))
        consts[-1].start()

    reach = 1 if ppd > 1 else 2
    barrier = pltpu.get_barrier_semaphore()
    for p in range(1, groups):
        pl.semaphore_signal(barrier, inc=1, device_id={"vel": lax.rem(me + p, groups)}, device_id_type=MESH)
    pl.semaphore_signal(barrier, inc=1, device_id={"space": ahead}, device_id_type=MESH)
    pl.semaphore_signal(barrier, inc=1, device_id={"space": behind}, device_id_type=MESH)
    for r in range(1, reach + 1):
        pl.semaphore_signal(barrier, inc=1, device_id=along(r), device_id_type=MESH)
        pl.semaphore_signal(barrier, inc=1, device_id=along(-r), device_id_type=MESH)
    pl.semaphore_wait(barrier, groups + 1 + 2 * reach)

    lane = lax.broadcasted_iota(jnp.int32, (1, LANES), 1)
    vy = (((lane // GZ) % GY).astype(jnp.float32) - 0.5 * (GY - 1)) * SPACING
    vz = ((lane % GZ).astype(jnp.float32) - 0.5 * (GZ - 1)) * SPACING
    block = (nz, LANES)
    pos_y = jnp.broadcast_to(vy > 0.0, block)
    pos_z = jnp.broadcast_to(vz > 0.0, block)
    half_y = jnp.broadcast_to(jnp.where(vy > 0.0, 0.5, -0.5), block)
    half_z = jnp.broadcast_to(jnp.where(vz > 0.0, 0.5, -0.5), block)
    rate_y = jnp.broadcast_to(COURANT * jnp.abs(vy), block)
    rate_z = jnp.broadcast_to(COURANT * jnp.abs(vz), block)

    def pick(positive, negative):
        return bit * positive + (1 - bit) * negative

    def across(value, emit):
        def y_state(mid, before, after):
            return mid + half_y * limited(before, after)

        f = {y: value(y) for y in range(-2, 2)}
        d = {y: f[y + 1] - f[y] for y in (-2, -1, 0)}
        cy = {y: y_state(f[y], d[y - 1], d[y]) for y in (-1, 0)}
        for y in range(hy):
            f[y + 2] = value(y + 2)
            d[y + 1] = f[y + 2] - f[y + 1]
            cy[y + 1] = y_state(f[y + 1], d[y], d[y + 1])
            mid = f[y]
            total = rate_y * (cy[y] - jnp.where(pos_y, cy[y - 1], cy[y + 1]))
            dz = pltpu.roll(mid, nz - 1, 0) - mid
            cz = mid + half_z * limited(pltpu.roll(dz, 1, 0), dz)
            total += rate_z * (cz - jnp.where(pos_z, pltpu.roll(cz, 1, 0), pltpu.roll(cz, nz - 1, 0)))
            emit(y, mid, total)

    def speed(tile):
        return COURANT * jnp.abs((tile.astype(jnp.float32) - 0.5 * (GX - 1)) * SPACING)

    def transport(dest, h):
        def row(y):
            return lax.rem(h * hy + y + ny, ny) * nz

        @pl.loop(0, tiles)
        def _(t):
            cols = pl.ds(pl.multiple_of(t * LANES, LANES), LANES)
            rate_x = speed(lax.div(me * width + t * LANES, GY * GZ))
            for j in range(ppd):
                index = 2 + dest * ppd + pick(j, ppd - 1 - j)

                def at(k, y):
                    return cur[pl.ds(pl.multiple_of(k * plane + row(y), nz), nz), cols]

                def emit(y, mid, total):
                    down, up = at(index + sign, y), at(index - sign, y)
                    cx = state(up, mid, down)
                    keep = pl.ds(y * nz, nz)
                    if j == 0:
                        before = state(at(index - 2 * sign, y), up, mid)
                    else:
                        before = cprev[keep]
                    if j < ppd - 1:
                        cprev[keep] = cx
                    result = mid - (total + rate_x * (cx - before))
                    sendbuf[index - 2, pl.ds(pl.multiple_of(row(y), nz), nz), cols] = result.astype(jnp.bfloat16)

                across(lambda y: at(index, y), emit)

    def own_lanes(v):
        return pl.ds(pl.multiple_of(v * width, width), width)

    def row_src(dest, h):
        return sendbuf.at[pl.ds(dest * ppd, ppd), pl.ds(pl.multiple_of(h * half, half), half)]

    def row_copy(dest, peer, r, h):
        return pltpu.make_async_remote_copy(
            src_ref=row_src(dest, h), dst_ref=recv.at[h, :, :, own_lanes(me)],
            send_sem=row_send.at[h, r], recv_sem=row_recv.at[h, r],
            device_id={"vel": peer}, device_id_type=MESH)

    def row_local(h):
        return pltpu.make_async_copy(row_src(mine, h), recv.at[h, :, :, own_lanes(me)], local_sem.at[0, h])

    def unit(dest, h):
        transport(dest, h)
        peer = vel_of(slab, dest)
        r = lax.rem(peer - me + groups, groups)

        @pl.when(r == 0)
        def _():
            row_local(h).start()

        @pl.when(r != 0)
        def _():
            row_copy(dest, peer, r, h).start()

    edge = 2 if ppd == 1 else 1
    mid_count = groups - 2 * edge
    early = mid_count // 2

    def mid_dest(k):
        return edge + lax.rem(mine + k, mid_count)

    def edge_dest(k):
        n = lax.rem(mine + k, 2 * edge)
        return n + lax.div(n, edge) * mid_count

    def row_list(h):
        out = []
        for r in range(1, groups):
            peer = lax.rem(me + r, groups)
            out.append(row_copy(chain_of(slab, peer), peer, r, h))
        return out

    def z_copies():
        return [
            pltpu.make_async_remote_copy(
                src_ref=zsend.at[pl.ds(0, 2 * plane)], dst_ref=zrecv.at[pl.ds(0, 2 * plane)],
                send_sem=z_send.at[0], recv_sem=z_recv.at[0], device_id={"space": ahead}, device_id_type=MESH),
            pltpu.make_async_remote_copy(
                src_ref=zsend.at[pl.ds(2 * plane, plane)], dst_ref=zrecv.at[pl.ds(2 * plane, plane)],
                send_sem=z_send.at[1], recv_sem=z_recv.at[1], device_id={"space": behind}, device_id_type=MESH),
        ]

    def prepare():
        own = ppd * plane
        span = 4 * LANES
        base = mine * (own // LANES)
        eye = lax.broadcasted_iota(jnp.int32, (nz, nz), 0) == lax.broadcasted_iota(jnp.int32, (nz, nz), 1)
        columns = {}
        for j in range(ppd):
            sheet = relax[mine * ppd + j]
            for h in range(HALVES):
                parts = []
                for y in range(hy):
                    line = jnp.broadcast_to(sheet[h * hy + y:h * hy + y + 1, :], (nz, nz))
                    one = jnp.sum(jnp.where(eye, line, 0.0), axis=1, keepdims=True)
                    parts.append(jnp.broadcast_to(one, (nz, LANES)))
                columns[h, j] = jnp.concatenate(parts, axis=0)
        for step in range(STEPS):
            count = counts[step, slab]
            flags = jnp.zeros((16, LANES), jnp.float32)
            for n in range(cells // span):
                which = kin_cells[step:step + 1, n * span:(n + 1) * span]
                live = n * span + lax.broadcasted_iota(jnp.int32, (1, span), 1) < count
                quotient = jnp.where(live, lax.div(which, LANES) - base, -1)
                hot_high = lax.broadcasted_iota(jnp.int32, (16, span), 0) == quotient
                hot_low = lax.broadcasted_iota(jnp.int32, (LANES, span), 0) == lax.rem(which, LANES)
                flags += lax.dot_general(
                    jnp.where(hot_high, 1.0, 0.0).astype(jnp.bfloat16), jnp.where(hot_low, 1.0, 0.0).astype(jnp.bfloat16),
                    (((1,), (1,)), ((), ())), preferred_element_type=jnp.float32)
            for j in range(ppd):
                for h in range(HALVES):
                    n = j * HALVES + h
                    kin = jnp.broadcast_to(flags[n:n + 1], (LANES, LANES)).T > 0.5
                    rate = columns[h, j]
                    here = pl.ds(j * half, half)
                    coef[step, 0, h, here] = jnp.where(kin, 1.0, 1.0 - rate)
                    coef[step, 1, h, here] = jnp.where(kin, COLLIDE, rate)
                    coef[step, 2, h, here] = jnp.where(kin, 1.0, 0.0)

    def wide(x):
        return jnp.concatenate([x] * (TILE // LANES), axis=1)

    def collide(step, h):
        rows = recv.at[h]

        def lhs():
            return rows[...].reshape(block_rows, nv)

        @pl.loop(0, rank // TILE)
        def _(n):
            cols = pl.ds(pl.multiple_of(n * TILE, TILE), TILE)
            first = jnp.dot(lhs(), map_a[:, cols], preferred_element_type=jnp.float32)
            second = jnp.dot(lhs(), map_b[:, cols], preferred_element_type=jnp.float32)
            hid[:, cols] = (first * second * wide(coef[step, 2, h])).astype(jnp.bfloat16)

        mom = jnp.dot(lhs(), basis[...], preferred_element_type=jnp.float32)
        high = mom.astype(jnp.bfloat16).astype(jnp.float32)
        is_low = (lax.broadcasted_iota(jnp.int32, mom.shape, 1) // 8) == 1
        split = jnp.where(is_low, mom - high, high)
        hid[:, rank:rank + LANES] = (split * (1.0 - coef[step, 2, h])).astype(jnp.bfloat16)

        @pl.loop(0, nv // TILE)
        def _(n):
            cols = pl.ds(pl.multiple_of(n * TILE, TILE), TILE)
            out = jnp.dot(hid[...], map_c[:, cols], preferred_element_type=jnp.float32)
            for j in range(ppd):
                part = slice(j * half, (j + 1) * half)
                here = pl.ds(h * half, half)
                if step == 0:
                    old = rows[j, :, cols].astype(jnp.float32)
                else:
                    old = mv[j, here, cols]
                new = wide(coef[step, 0, h, part]) * old + wide(coef[step, 1, h, part]) * out[part]
                if step == 0:
                    fown[j, here, cols] = new
                    fsend[h, j, :, cols] = new.astype(jnp.bfloat16)
                else:
                    outbuf[h, j, :, cols] = new.astype(jnp.bfloat16)

    low, high_part = pl.ds(0, nv // 2), pl.ds(nv // 2, nv // 2)
    whole = pl.ds(0, nv)

    def halo_copies(h):
        out = []
        for k, (j, r, lanes) in enumerate((
                (reach * ppd - 2, reach, high_part), (ppd - 1, 1, whole), (0, -1, whole), (ppd + 1 - reach * ppd, -reach, low))):
            out.append(pltpu.make_async_remote_copy(
                src_ref=fsend.at[h, j, :, lanes], dst_ref=halo.at[h, k, :, lanes],
                send_sem=halo_send.at[h, k], recv_sem=halo_recv.at[h, k],
                device_id=along(r), device_id_type=MESH))
        return out

    def sideways(h):
        @pl.loop(0, nv // LANES)
        def _(t):
            cols = pl.ds(pl.multiple_of(t * LANES, LANES), LANES)
            for j in range(ppd):
                def emit(y, mid, total):
                    mv[j, pl.ds((h * hy + y) * nz, nz), cols] = mid - total

                across(lambda y: fown[j, pl.ds(((h * hy + y) % ny) * nz, nz), cols], emit)

    def forward(h):
        half_tiles = nv // LANES // 2
        for up in (-1, 1):
            @pl.loop(0, half_tiles)
            def _(n):
                t = n + (half_tiles if up > 0 else 0)
                cols = pl.ds(pl.multiple_of(t * LANES, LANES), LANES)
                rate_x = speed(t)

                def value(k, y):
                    here = pl.ds(y * nz, nz)
                    if 0 <= k < ppd:
                        return fown[k, pl.ds((h * hy + y) * nz, nz), cols]
                    slot = k + 2 if k < 0 else k - ppd + 2
                    return halo[h, slot, here, cols].astype(jnp.float32)

                order = list(range(ppd)) if up > 0 else list(range(ppd - 1, -1, -1))
                for y in range(hy):
                    line = [order[0] - 2 * up, order[0] - up] + order + [order[-1] + up]
                    f = [value(k, y) for k in line]
                    c = [state(f[n], f[n + 1], f[n + 2]) for n in range(ppd + 1)]
                    here = pl.ds((h * hy + y) * nz, nz)
                    for n, j in enumerate(order):
                        result = mv[j, here, cols] - rate_x * (c[n + 1] - c[n])
                        mv[j, here, cols] = result
                        recv[h, j, pl.ds(y * nz, nz), cols] = result.astype(jnp.bfloat16)

    def res_copies(h):
        out = []
        for r in range(1, groups):
            peer = lax.rem(me + r, groups)
            out.append(pltpu.make_async_remote_copy(
                src_ref=outbuf.at[h, :, :, own_lanes(peer)],
                dst_ref=ret_out.at[pl.ds(mine * ppd, ppd), pl.ds(h * half, half)],
                send_sem=res_send.at[h, r], recv_sem=res_recv.at[h, r],
                device_id={"vel": peer}, device_id_type=MESH))
        return out

    def res_local(h):
        return pltpu.make_async_copy(
            outbuf.at[h, :, :, own_lanes(me)],
            ret_out.at[pl.ds(mine * ppd, ppd), pl.ds(h * half, half)], local_sem.at[1, h])

    for copy in loads:
        copy.wait()
    two, one = 2 * plane, plane
    zsend[pl.ds(0, two)] = cur[pl.ds(pl.multiple_of(pick(nx * plane, two), plane), two)].astype(jnp.bfloat16)
    zsend[pl.ds(two, one)] = cur[pl.ds(pl.multiple_of(pick(two, (nx + 1) * plane), plane), one)].astype(jnp.bfloat16)
    z_list = z_copies()
    for copy in z_list:
        copy.start()

    @pl.loop(0, mid_count + early)
    def _(k):
        h = lax.div(k, mid_count)
        unit(mid_dest(k - h * mid_count), h)

    prepare()
    for copy in z_list:
        copy.wait_recv()
    cur[pl.ds(pl.multiple_of(pick(0, (nx + 2) * plane), plane), two)] = zrecv[pl.ds(0, two)].astype(jnp.float32)
    cur[pl.ds(pl.multiple_of(pick((nx + 2) * plane, plane), plane), one)] = zrecv[pl.ds(two, one)].astype(jnp.float32)

    @pl.loop(0, 4 * edge + mid_count - early)
    def _(k):
        h = jnp.where(k < 2 * edge, 0, 1)
        n = k - h * 2 * edge
        rest = mid_count - early
        at_mid = h * jnp.where(n < rest, 1, 0)
        e = n - h * rest
        dest = at_mid * mid_dest(early + n) + (1 - at_mid) * edge_dest(e + 2 * edge * at_mid + rest * at_mid)
        unit(dest, h)

    for copy in consts:
        copy.wait()
    rows_in = [row_list(h) for h in range(HALVES)]
    halos = [halo_copies(h) for h in range(HALVES)]
    results = [res_copies(h) for h in range(HALVES)]
    for h in range(HALVES):
        for copy in rows_in[h]:
            copy.wait_recv()
        row_local(h).wait()
        collide(0, h)
        for copy in halos[h]:
            copy.start()
    for h in range(HALVES):
        sideways(h)
        for copy in halos[h]:
            copy.wait_recv()
        forward(h)
        collide(1, h)
        for copy in results[h]:
            copy.start()
        res_local(h).start()
    for copy in z_list:
        copy.wait_send()
    for h in range(HALVES):
        for copy in rows_in[h] + halos[h]:
            copy.wait_send()
        for copy in results[h]:
            copy.wait()
        res_local(h).wait()


def body(dist, relax_rate, kinetic_cells, kinetic_count, map_a, map_b, map_c):
    nx, ny, nz, width = dist.shape
    groups = lax.axis_size("vel")
    slabs = lax.axis_size("space")
    cells = nx * ny * nz
    plane = ny * nz
    nv = groups * width
    rank = map_a.shape[1]
    ppd = nx // groups
    half = plane // HALVES
    basis, back = tables()

    any_space = pl.BlockSpec(memory_space=pl.ANY)
    f32, bf16 = jnp.float32, jnp.bfloat16
    dims = (nx, ny, nz, width, groups, slabs)
    vmem = pl.BlockSpec(memory_space=pltpu.VMEM)
    dma = pltpu.SemaphoreType.DMA
    ret = pl.pallas_call(
        functools.partial(kernel, dims),
        out_shape=jax.ShapeDtypeStruct((nx, plane, width), bf16),
        in_specs=[pl.BlockSpec(memory_space=pltpu.SMEM)] + [vmem] * 2 + [any_space] * 6,
        out_specs=any_space,
        scratch_shapes=[
            pltpu.VMEM(((nx + 4) * plane, width), f32),
            pltpu.VMEM((half, LANES), f32),
            pltpu.VMEM((nx, plane, width), bf16),
            pltpu.VMEM((3 * plane, width), bf16),
            pltpu.VMEM((3 * plane, width), bf16),
            pltpu.VMEM((HALVES, ppd, half, nv), bf16),
            pltpu.VMEM((ppd, plane, nv), f32),
            pltpu.VMEM((HALVES, ppd, half, nv), bf16),
            pltpu.VMEM((HALVES, 4, half, nv), bf16),
            pltpu.VMEM((ppd, plane, nv), f32),
            pltpu.VMEM((HALVES, ppd, half, nv), bf16),
            pltpu.VMEM(map_a.shape, bf16),
            pltpu.VMEM(map_b.shape, bf16),
            pltpu.VMEM((rank + LANES, nv), bf16),
            pltpu.VMEM((nv, LANES), bf16),
            pltpu.VMEM((ppd * half, rank + LANES), bf16),
            pltpu.VMEM((STEPS, 3, HALVES, ppd * half, LANES), f32),
            dma((4,)),
            dma((5,)),
            dma((2, HALVES)),
            dma((2,)),
            dma((2,)),
            dma((HALVES, groups)),
            dma((HALVES, groups)),
            dma((HALVES, 4)),
            dma((HALVES, 4)),
            dma((HALVES, groups)),
            dma((HALVES, groups)),
        ],
        compiler_params=pltpu.CompilerParams(
            collective_id=0, has_side_effects=True, vmem_limit_bytes=67043328),
    )(kinetic_count, kinetic_cells, relax_rate, dist.reshape(cells, width), map_a, map_b, map_c,
      jnp.asarray(basis), jnp.asarray(back))
    return ret.reshape(dist.shape).astype(f32)


def solution(mesh):
    return jax.shard_map(
        body,
        mesh=mesh,
        in_specs=(
            P("space", None, None, "vel"),
            P("space", None, None),
            P(None, "space"),
            P(),
            P(),
            P(),
            P(),
        ),
        out_specs=P("space", None, None, "vel"),
        check_vma=False,
    )
```

time: 125 us -> 81.9 us (0.66)
  Pallas kernels: 122 us -> 77.5 us
  other arithmetic: 0 us -> 4.19 us
  local copies, waits for them, and re-layouts: 2.94 us -> 0 us
    pallas_call x2 -> x1, Pallas kernels: 122 us -> 77.5 us  [body(): pl.pallas_call(functools.partial(kernel, dims), out_shape=jax.ShapeDtypeS...]
    convert_element_type x0 -> x1, other arithmetic: none -> 4.19 us  [body(): return ret.reshape(dist.shape).astype(f32)]
    reshape x1 -> x0, local copies, waits for them, and re-layouts: 1.61 us -> none  [body(): relax_rate.reshape(cells // LANES, LANES)]
where the time goes in v1:
time: 81.9 us; the launch traced here: 81.7 us
  Pallas kernels  77.5 us (95%)
  other arithmetic  4.19 us (5%)
    pallas_call x1, Pallas kernels, body(): pl.pallas_call(functools.partial(kernel, dims), out_shape=jax.ShapeDtypeS...  77.5 us
    convert_element_type x1, other arithmetic, body(): return ret.reshape(dist.shape).astype(f32)  4.19 us

profile of v1, /device:TPU:1, one launch (start us, length us, event | category | flops | bytes accessed | tf_op | source)
XLA Modules:
  0.0 81.7 jit_solution(845372297906040384)
XLA Ops:
  0.0 77.5 %shard_map.91 = bf16[16,256,256]{2,1,0:T(8,128)(2,1)} custom-call(s32[2,4]{1,0:T(2,128)} %counts.1, s32[2,4096]{1,0:T(2,128)} %kin_cells.1, f32[16,16,16]{2,1,0:T(8,128)} %relax.1, f32[4096,256]{1,0:T(8,128)} %bitcast.4, bf16[2048,768]{1,0:T(8,128)(2,1)} %a_hbm.1, bf16[2048,768]{1,0:T(8,128)(2,1)} %b_hbm.1, bf16[768,2048]{1,0:T(8,128)(2,1)} %c_hbm.1, ...), custom_call_target="tpu_custom_call" | custom-call | tf_op jit(solution)/shard_map/pallas_call | solution.py:473
  77.5 4.2 %convert.1 = f32[16,16,16,256]{3,2,1,0:T(8,128)} convert(bf16[16,16,16,256]{3,2,1,0:T(8,128)(2,1)} %bitcast.3) | non-fusion elementwise | flops 1048576 | bytes 6291456 | tf_op jit(solution)/shard_map/convert_element_type | solution.py:512

commit v2 on v1

--- a/solution.py
+++ b/solution.py
@@ -107,16 +107,15 @@
 
     pieces = 4
     loads = []
-    for c in range(pieces):
+    for n, c in enumerate((0, pieces - 1) + tuple(range(1, pieces - 1))):
         size = cells // pieces
         loads.append(pltpu.make_async_copy(
-            dist.at[pl.ds(c * size, size)], cur.at[pl.ds(2 * plane + c * size, size)], load_sem.at[c]))
+            dist.at[pl.ds(c * size, size)], cur.at[pl.ds(2 * plane + c * size, size)], load_sem.at[n]))
         loads[-1].start()
     consts = []
     for n, (src, dst) in enumerate(((a_hbm, map_a), (b_hbm, map_b), (c_hbm, map_c.at[pl.ds(0, rank)]),
                                     (back_hbm, map_c.at[pl.ds(rank, LANES)]), (basis_hbm, basis))):
         consts.append(pltpu.make_async_copy(src, dst, const_sem.at[n]))
-        consts[-1].start()
 
     reach = 1 if ppd > 1 else 2
     barrier = pltpu.get_barrier_semaphore()
@@ -127,7 +126,6 @@
     for r in range(1, reach + 1):
         pl.semaphore_signal(barrier, inc=1, device_id=along(r), device_id_type=MESH)
         pl.semaphore_signal(barrier, inc=1, device_id=along(-r), device_id_type=MESH)
-    pl.semaphore_wait(barrier, groups + 1 + 2 * reach)
 
     lane = lax.broadcasted_iota(jnp.int32, (1, LANES), 1)
     vy = (((lane // GZ) % GY).astype(jnp.float32) - 0.5 * (GY - 1)) * SPACING
@@ -223,7 +221,7 @@
 
     edge = 2 if ppd == 1 else 1
     mid_count = groups - 2 * edge
-    early = mid_count // 2
+    far_count = groups - 4 * edge
 
     def mid_dest(k):
         return edge + lax.rem(mine + k, mid_count)
@@ -231,6 +229,16 @@
     def edge_dest(k):
         n = lax.rem(mine + k, 2 * edge)
         return n + lax.div(n, edge) * mid_count
+
+    def near_dest(k):
+        n = lax.rem(mine + k, 2 * edge)
+        return edge + n + lax.div(n, edge) * far_count
+
+    def late_dest(k):
+        n = lax.rem(mine + k, mid_count)
+        first = jnp.where(n < edge, 1, 0)
+        last = jnp.where(n >= mid_count - edge, 1, 0)
+        return first * n + last * (n + 2 * edge) + (1 - first - last) * (n + edge)
 
     def row_list(h):
         out = []
@@ -392,19 +400,24 @@
             outbuf.at[h, :, :, own_lanes(me)],
             ret_out.at[pl.ds(mine * ppd, ppd), pl.ds(h * half, half)], local_sem.at[1, h])
 
-    for copy in loads:
+    for copy in loads[:2]:
         copy.wait()
     two, one = 2 * plane, plane
     zsend[pl.ds(0, two)] = cur[pl.ds(pl.multiple_of(pick(nx * plane, two), plane), two)].astype(jnp.bfloat16)
     zsend[pl.ds(two, one)] = cur[pl.ds(pl.multiple_of(pick(two, (nx + 1) * plane), plane), one)].astype(jnp.bfloat16)
     z_list = z_copies()
+    pl.semaphore_wait(barrier, groups + 1 + 2 * reach)
     for copy in z_list:
         copy.start()
-
-    @pl.loop(0, mid_count + early)
+    for copy in loads[2:]:
+        copy.wait()
+    for copy in consts:
+        copy.start()
+
+    @pl.loop(0, mid_count + 2 * edge)
     def _(k):
         h = lax.div(k, mid_count)
-        unit(mid_dest(k - h * mid_count), h)
+        unit((1 - h) * mid_dest(k) + h * near_dest(k), h)
 
     prepare()
     for copy in z_list:
@@ -412,15 +425,10 @@
     cur[pl.ds(pl.multiple_of(pick(0, (nx + 2) * plane), plane), two)] = zrecv[pl.ds(0, two)].astype(jnp.float32)
     cur[pl.ds(pl.multiple_of(pick((nx + 2) * plane, plane), plane), one)] = zrecv[pl.ds(two, one)].astype(jnp.float32)
 
-    @pl.loop(0, 4 * edge + mid_count - early)
+    @pl.loop(0, mid_count + 2 * edge)
     def _(k):
         h = jnp.where(k < 2 * edge, 0, 1)
-        n = k - h * 2 * edge
-        rest = mid_count - early
-        at_mid = h * jnp.where(n < rest, 1, 0)
-        e = n - h * rest
-        dest = at_mid * mid_dest(early + n) + (1 - at_mid) * edge_dest(e + 2 * edge * at_mid + rest * at_mid)
-        unit(dest, h)
+        unit((1 - h) * edge_dest(k) + h * late_dest(k), h)
 
     for copy in consts:
         copy.wait()
@@ -509,7 +517,35 @@
             collective_id=0, has_side_effects=True, vmem_limit_bytes=67043328),
     )(kinetic_count, kinetic_cells, relax_rate, dist.reshape(cells, width), map_a, map_b, map_c,
       jnp.asarray(basis), jnp.asarray(back))
-    return ret.reshape(dist.shape).astype(f32)
+    parts = 16
+    out = pl.pallas_call(
+        widen,
+        out_shape=jax.ShapeDtypeStruct((cells, width), f32),
+        in_specs=[any_space],
+        out_specs=any_space,
+        scratch_shapes=[
+            pltpu.VMEM((parts, cells // parts, width), bf16),
+            pltpu.VMEM((parts, cells // parts, width), f32),
+            dma((parts,)),
+            dma((parts,)),
+        ],
+    )(ret.reshape(cells, width))
+    return out.reshape(dist.shape)
+
+
+def widen(src, out, buf, wide_buf, in_sem, out_sem):
+    parts = in_sem.shape[0]
+    size = src.shape[0] // parts
+    ins = [pltpu.make_async_copy(src.at[pl.ds(n * size, size)], buf.at[n], in_sem.at[n]) for n in range(parts)]
+    outs = [pltpu.make_async_copy(wide_buf.at[n], out.at[pl.ds(n * size, size)], out_sem.at[n]) for n in range(parts)]
+    for copy in ins:
+        copy.start()
+    for n in range(parts):
+        ins[n].wait()
+        wide_buf[n] = buf[n].astype(jnp.float32)
+        outs[n].start()
+    for copy in outs:
+        copy.wait()
 
 
 def solution(mesh):

time: 81.9 us -> 75.6 us (0.923)
  other arithmetic: 4.19 us -> 0 us
  Pallas kernels: 77.5 us -> 75.4 us
    pallas_call x1, Pallas kernels: 77.5 us -> 72.2 us  [body(): pl.pallas_call(functools.partial(kernel, dims), out_shape=jax.ShapeDtypeS...]
    convert_element_type x1 -> x0, other arithmetic: 4.19 us -> none  [body(): return ret.reshape(dist.shape).astype(f32)]
    pallas_call x0 -> x1, Pallas kernels: none -> 3.2 us  [body(): pl.pallas_call(widen, out_shape=jax.ShapeDtypeStruct((cells, width), f32)...]
where the time goes in v2:
time: 75.6 us; the launch traced here: 75.4 us
  Pallas kernels  75.4 us (100%)
    pallas_call x1, Pallas kernels, body(): pl.pallas_call(functools.partial(kernel, dims), out_shape=jax.ShapeDtypeS...  72.2 us
    pallas_call x1, Pallas kernels, body(): pl.pallas_call(widen, out_shape=jax.ShapeDtypeStruct((cells, width), f32)...  3.2 us

profile of v2, /device:TPU:1, one launch (start us, length us, event | category | flops | bytes accessed | tf_op | source)
XLA Modules:
  0.0 75.4 jit_solution(10891015417449412167)
XLA Ops:
  0.0 72.2 %shard_map.91 = bf16[16,256,256]{2,1,0:T(8,128)(2,1)} custom-call(s32[2,4]{1,0:T(2,128)} %counts.1, s32[2,4096]{1,0:T(2,128)} %kin_cells.1, f32[16,16,16]{2,1,0:T(8,128)} %relax.1, f32[4096,256]{1,0:T(8,128)} %bitcast.4, bf16[2048,768]{1,0:T(8,128)(2,1)} %a_hbm.1, bf16[2048,768]{1,0:T(8,128)(2,1)} %b_hbm.1, bf16[768,2048]{1,0:T(8,128)(2,1)} %c_hbm.1, ...), custom_call_target="tpu_custom_call" | custom-call | tf_op jit(solution)/shard_map/pallas_call | solution.py:481
  72.2 3.2 %shard_map.92 = f32[4096,256]{1,0:T(8,128)} custom-call(bf16[4096,256]{1,0:T(8,128)(2,1)} %bitcast.3), custom_call_target="tpu_custom_call" | custom-call | tf_op jit(solution)/shard_map/pallas_call | solution.py:521

commit v3 on v2

--- a/solution.py
+++ b/solution.py
@@ -60,10 +60,10 @@
     return mid + 0.5 * limited(mid - up, down - mid)
 
 
-def kernel(dims, counts, kin_cells, relax, dist, a_hbm, b_hbm, c_hbm, basis_hbm, back_hbm,
+def kernel(dims, counts_hbm, kin_hbm, relax_hbm, dist, a_hbm, b_hbm, c_hbm, basis_hbm, back_hbm,
            ret_out,
            cur, cprev, sendbuf, zsend, zrecv, recv, fown, fsend, halo, mv, outbuf,
-           map_a, map_b, map_c, basis, hid, coef,
+           map_a, map_b, map_c, basis, hid, coef, counts, kin_cells, relax,
            load_sem, const_sem, local_sem, z_send, z_recv, row_send, row_recv, halo_send, halo_recv, res_send, res_recv):
     nx, ny, nz, width, groups, slabs = dims
     plane = ny * nz
@@ -105,6 +105,16 @@
         s = lax.rem(slab + lax.div(at, groups) - 1 + slabs, slabs)
         return {"space": s, "vel": vel_of(s, lax.rem(at, groups))}
 
+    reach = 1 if ppd > 1 else 2
+    barrier = pltpu.get_barrier_semaphore()
+    for p in range(1, groups):
+        pl.semaphore_signal(barrier, inc=1, device_id={"vel": lax.rem(me + p, groups)}, device_id_type=MESH)
+    pl.semaphore_signal(barrier, inc=1, device_id={"space": ahead}, device_id_type=MESH)
+    pl.semaphore_signal(barrier, inc=1, device_id={"space": behind}, device_id_type=MESH)
+    for r in range(1, reach + 1):
+        pl.semaphore_signal(barrier, inc=1, device_id=along(r), device_id_type=MESH)
+        pl.semaphore_signal(barrier, inc=1, device_id=along(-r), device_id_type=MESH)
+
     pieces = 4
     loads = []
     for n, c in enumerate((0, pieces - 1) + tuple(range(1, pieces - 1))):
@@ -114,18 +124,9 @@
         loads[-1].start()
     consts = []
     for n, (src, dst) in enumerate(((a_hbm, map_a), (b_hbm, map_b), (c_hbm, map_c.at[pl.ds(0, rank)]),
-                                    (back_hbm, map_c.at[pl.ds(rank, LANES)]), (basis_hbm, basis))):
+                                    (back_hbm, map_c.at[pl.ds(rank, LANES)]), (basis_hbm, basis),
+                                    (counts_hbm, counts), (kin_hbm, kin_cells), (relax_hbm, relax))):
         consts.append(pltpu.make_async_copy(src, dst, const_sem.at[n]))
-
-    reach = 1 if ppd > 1 else 2
-    barrier = pltpu.get_barrier_semaphore()
-    for p in range(1, groups):
-        pl.semaphore_signal(barrier, inc=1, device_id={"vel": lax.rem(me + p, groups)}, device_id_type=MESH)
-    pl.semaphore_signal(barrier, inc=1, device_id={"space": ahead}, device_id_type=MESH)
-    pl.semaphore_signal(barrier, inc=1, device_id={"space": behind}, device_id_type=MESH)
-    for r in range(1, reach + 1):
-        pl.semaphore_signal(barrier, inc=1, device_id=along(r), device_id_type=MESH)
-        pl.semaphore_signal(barrier, inc=1, device_id=along(-r), device_id_type=MESH)
 
     lane = lax.broadcasted_iota(jnp.int32, (1, LANES), 1)
     vy = (((lane // GZ) % GY).astype(jnp.float32) - 0.5 * (GY - 1)) * SPACING
@@ -141,14 +142,14 @@
     def pick(positive, negative):
         return bit * positive + (1 - bit) * negative
 
-    def across(value, emit):
+    def across(value, emit, first, last):
         def y_state(mid, before, after):
             return mid + half_y * limited(before, after)
 
-        f = {y: value(y) for y in range(-2, 2)}
-        d = {y: f[y + 1] - f[y] for y in (-2, -1, 0)}
-        cy = {y: y_state(f[y], d[y - 1], d[y]) for y in (-1, 0)}
-        for y in range(hy):
+        f = {y: value(y) for y in range(first - 2, first + 2)}
+        d = {y: f[y + 1] - f[y] for y in range(first - 2, first + 1)}
+        cy = {y: y_state(f[y], d[y - 1], d[y]) for y in (first - 1, first)}
+        for y in range(first, last):
             f[y + 2] = value(y + 2)
             d[y + 1] = f[y + 2] - f[y + 1]
             cy[y + 1] = y_state(f[y + 1], d[y], d[y + 1])
@@ -189,7 +190,7 @@
                     result = mid - (total + rate_x * (cx - before))
                     sendbuf[index - 2, pl.ds(pl.multiple_of(row(y), nz), nz), cols] = result.astype(jnp.bfloat16)
 
-                across(lambda y: at(index, y), emit)
+                across(lambda y: at(index, y), emit, 0, hy)
 
     def own_lanes(v):
         return pl.ds(pl.multiple_of(v * width, width), width)
@@ -208,6 +209,9 @@
 
     def unit(dest, h):
         transport(dest, h)
+        send(dest, h)
+
+    def send(dest, h):
         peer = vel_of(slab, dest)
         r = lax.rem(peer - me + groups, groups)
 
@@ -234,11 +238,8 @@
         n = lax.rem(mine + k, 2 * edge)
         return edge + n + lax.div(n, edge) * far_count
 
-    def late_dest(k):
-        n = lax.rem(mine + k, mid_count)
-        first = jnp.where(n < edge, 1, 0)
-        last = jnp.where(n >= mid_count - edge, 1, 0)
-        return first * n + last * (n + 2 * edge) + (1 - first - last) * (n + edge)
+    def far_dest(k):
+        return 2 * edge + lax.rem(mine + k, far_count)
 
     def row_list(h):
         out = []
@@ -247,15 +248,23 @@
             out.append(row_copy(chain_of(slab, peer), peer, r, h))
         return out
 
-    def z_copies():
+    def z_copies(h):
+        here = pl.ds(h * half, half)
         return [
             pltpu.make_async_remote_copy(
-                src_ref=zsend.at[pl.ds(0, 2 * plane)], dst_ref=zrecv.at[pl.ds(0, 2 * plane)],
-                send_sem=z_send.at[0], recv_sem=z_recv.at[0], device_id={"space": ahead}, device_id_type=MESH),
+                src_ref=zsend.at[pl.ds(0, 2), here], dst_ref=zrecv.at[pl.ds(0, 2), here],
+                send_sem=z_send.at[h, 0], recv_sem=z_recv.at[h, 0], device_id={"space": ahead}, device_id_type=MESH),
             pltpu.make_async_remote_copy(
-                src_ref=zsend.at[pl.ds(2 * plane, plane)], dst_ref=zrecv.at[pl.ds(2 * plane, plane)],
-                send_sem=z_send.at[1], recv_sem=z_recv.at[1], device_id={"space": behind}, device_id_type=MESH),
+                src_ref=zsend.at[pl.ds(2, 1), here], dst_ref=zrecv.at[pl.ds(2, 1), here],
+                send_sem=z_send.at[h, 1], recv_sem=z_recv.at[h, 1], device_id={"space": behind}, device_id_type=MESH),
         ]
+
+    def z_place(h):
+        for copy in z_list[h]:
+            copy.wait_recv()
+        for n, at in enumerate((pick(0, nx + 2), pick(1, nx + 3), pick(nx + 2, 1))):
+            here = pl.ds(pl.multiple_of(at * plane + h * half, half), half)
+            cur[here] = zrecv[n, h * half:(h + 1) * half].astype(jnp.float32)
 
     def prepare():
         own = ppd * plane
@@ -347,7 +356,7 @@
                 device_id=along(r), device_id_type=MESH))
         return out
 
-    def sideways(h):
+    def sideways(h, spans):
         @pl.loop(0, nv // LANES)
         def _(t):
             cols = pl.ds(pl.multiple_of(t * LANES, LANES), LANES)
@@ -355,7 +364,8 @@
                 def emit(y, mid, total):
                     mv[j, pl.ds((h * hy + y) * nz, nz), cols] = mid - total
 
-                across(lambda y: fown[j, pl.ds(((h * hy + y) % ny) * nz, nz), cols], emit)
+                for first, last in spans:
+                    across(lambda y: fown[j, pl.ds(((h * hy + y) % ny) * nz, nz), cols], emit, first, last)
 
     def forward(h):
         half_tiles = nv // LANES // 2
@@ -402,39 +412,46 @@
 
     for copy in loads[:2]:
         copy.wait()
-    two, one = 2 * plane, plane
-    zsend[pl.ds(0, two)] = cur[pl.ds(pl.multiple_of(pick(nx * plane, two), plane), two)].astype(jnp.bfloat16)
-    zsend[pl.ds(two, one)] = cur[pl.ds(pl.multiple_of(pick(two, (nx + 1) * plane), plane), one)].astype(jnp.bfloat16)
-    z_list = z_copies()
-    pl.semaphore_wait(barrier, groups + 1 + 2 * reach)
-    for copy in z_list:
-        copy.start()
+    for n, at in enumerate((pick(nx, 2), pick(nx + 1, 3), pick(2, nx + 1))):
+        zsend[n] = cur[pl.ds(pl.multiple_of(at * plane, plane), plane)].astype(jnp.bfloat16)
+    z_list = [z_copies(h) for h in range(HALVES)]
     for copy in loads[2:]:
         copy.wait()
+    transport(mid_dest(0), 0)
+    pl.semaphore_wait(barrier, groups + 1 + 2 * reach)
+    for copy in z_list[0] + z_list[1]:
+        copy.start()
+    send(mid_dest(0), 0)
     for copy in consts:
         copy.start()
 
-    @pl.loop(0, mid_count + 2 * edge)
+    @pl.loop(1, mid_count + 2 * edge)
     def _(k):
         h = lax.div(k, mid_count)
         unit((1 - h) * mid_dest(k) + h * near_dest(k), h)
 
+    for copy in consts[5:]:
+        copy.wait()
     prepare()
-    for copy in z_list:
-        copy.wait_recv()
-    cur[pl.ds(pl.multiple_of(pick(0, (nx + 2) * plane), plane), two)] = zrecv[pl.ds(0, two)].astype(jnp.float32)
-    cur[pl.ds(pl.multiple_of(pick((nx + 2) * plane, plane), plane), one)] = zrecv[pl.ds(two, one)].astype(jnp.float32)
-
-    @pl.loop(0, mid_count + 2 * edge)
+    z_place(0)
+
+    @pl.loop(0, 2 * edge + far_count)
     def _(k):
         h = jnp.where(k < 2 * edge, 0, 1)
-        unit((1 - h) * edge_dest(k) + h * late_dest(k), h)
-
-    for copy in consts:
+        unit((1 - h) * edge_dest(k) + h * far_dest(k), h)
+
+    z_place(1)
+
+    @pl.loop(0, 2 * edge)
+    def _(k):
+        unit(edge_dest(k), 1)
+
+    for copy in consts[:5]:
         copy.wait()
     rows_in = [row_list(h) for h in range(HALVES)]
     halos = [halo_copies(h) for h in range(HALVES)]
     results = [res_copies(h) for h in range(HALVES)]
+    inner, outer = [(2, hy - 2)], [(0, 2), (hy - 2, hy)]
     for h in range(HALVES):
         for copy in rows_in[h]:
             copy.wait_recv()
@@ -442,8 +459,10 @@
         collide(0, h)
         for copy in halos[h]:
             copy.start()
+        if h < HALVES - 1:
+            sideways(h, inner)
     for h in range(HALVES):
-        sideways(h)
+        sideways(h, outer if h < HALVES - 1 else [(0, hy)])
         for copy in halos[h]:
             copy.wait_recv()
         forward(h)
@@ -451,10 +470,8 @@
         for copy in results[h]:
             copy.start()
         res_local(h).start()
-    for copy in z_list:
-        copy.wait_send()
     for h in range(HALVES):
-        for copy in rows_in[h] + halos[h]:
+        for copy in z_list[h] + rows_in[h] + halos[h]:
             copy.wait_send()
         for copy in results[h]:
             copy.wait()
@@ -480,15 +497,15 @@
     dma = pltpu.SemaphoreType.DMA
     ret = pl.pallas_call(
         functools.partial(kernel, dims),
-        out_shape=jax.ShapeDtypeStruct((nx, plane, width), bf16),
-        in_specs=[pl.BlockSpec(memory_space=pltpu.SMEM)] + [vmem] * 2 + [any_space] * 6,
-        out_specs=any_space,
+        out_shape=pltpu.VMEM((nx, plane, width), bf16),
+        in_specs=[any_space] * 9,
+        out_specs=vmem,
         scratch_shapes=[
             pltpu.VMEM(((nx + 4) * plane, width), f32),
             pltpu.VMEM((half, LANES), f32),
             pltpu.VMEM((nx, plane, width), bf16),
-            pltpu.VMEM((3 * plane, width), bf16),
-            pltpu.VMEM((3 * plane, width), bf16),
+            pltpu.VMEM((3, plane, width), bf16),
+            pltpu.VMEM((3, plane, width), bf16),
             pltpu.VMEM((HALVES, ppd, half, nv), bf16),
             pltpu.VMEM((ppd, plane, nv), f32),
             pltpu.VMEM((HALVES, ppd, half, nv), bf16),
@@ -501,11 +518,14 @@
             pltpu.VMEM((nv, LANES), bf16),
             pltpu.VMEM((ppd * half, rank + LANES), bf16),
             pltpu.VMEM((STEPS, 3, HALVES, ppd * half, LANES), f32),
+            pltpu.SMEM(kinetic_count.shape, jnp.int32),
+            pltpu.VMEM(kinetic_cells.shape, jnp.int32),
+            pltpu.VMEM(relax_rate.shape, f32),
             dma((4,)),
-            dma((5,)),
+            dma((8,)),
             dma((2, HALVES)),
-            dma((2,)),
-            dma((2,)),
+            dma((HALVES, 2)),
+            dma((HALVES, 2)),
             dma((HALVES, groups)),
             dma((HALVES, groups)),
             dma((HALVES, 4)),
@@ -514,35 +534,30 @@
             dma((HALVES, groups)),
         ],
         compiler_params=pltpu.CompilerParams(
-            collective_id=0, has_side_effects=True, vmem_limit_bytes=67043328),
+            collective_id=0, has_side_effects=True, vmem_limit_bytes=64880640),
     )(kinetic_count, kinetic_cells, relax_rate, dist.reshape(cells, width), map_a, map_b, map_c,
       jnp.asarray(basis), jnp.asarray(back))
     parts = 16
     out = pl.pallas_call(
         widen,
         out_shape=jax.ShapeDtypeStruct((cells, width), f32),
-        in_specs=[any_space],
+        in_specs=[vmem],
         out_specs=any_space,
         scratch_shapes=[
-            pltpu.VMEM((parts, cells // parts, width), bf16),
             pltpu.VMEM((parts, cells // parts, width), f32),
             dma((parts,)),
-            dma((parts,)),
         ],
+        compiler_params=pltpu.CompilerParams(vmem_limit_bytes=16 << 20),
     )(ret.reshape(cells, width))
     return out.reshape(dist.shape)
 
 
-def widen(src, out, buf, wide_buf, in_sem, out_sem):
-    parts = in_sem.shape[0]
+def widen(src, out, wide_buf, out_sem):
+    parts = out_sem.shape[0]
     size = src.shape[0] // parts
-    ins = [pltpu.make_async_copy(src.at[pl.ds(n * size, size)], buf.at[n], in_sem.at[n]) for n in range(parts)]
     outs = [pltpu.make_async_copy(wide_buf.at[n], out.at[pl.ds(n * size, size)], out_sem.at[n]) for n in range(parts)]
-    for copy in ins:
-        copy.start()
     for n in range(parts):
-        ins[n].wait()
-        wide_buf[n] = buf[n].astype(jnp.float32)
+        wide_buf[n] = src[n * size:(n + 1) * size].astype(jnp.float32)
         outs[n].start()
     for copy in outs:
         copy.wait()

time: 75.6 us -> 72.5 us (0.959)
  Pallas kernels: 75.4 us -> 72.3 us
    pallas_call x1, Pallas kernels: 72.2 us -> 70.2 us  [body(): pl.pallas_call(functools.partial(kernel, dims), out_shape=pltpu.VMEM((nx,...]
    pallas_call x1, Pallas kernels: 3.2 us -> 2.15 us  [body(): pl.pallas_call(widen, out_shape=jax.ShapeDtypeStruct((cells, width), f32)...]
where the time goes in v3:
time: 72.5 us; the launch traced here: 72.3 us
  Pallas kernels  72.3 us (100%)
    pallas_call x1, Pallas kernels, body(): pl.pallas_call(functools.partial(kernel, dims), out_shape=pltpu.VMEM((nx,...  70.2 us
    pallas_call x1, Pallas kernels, body(): pl.pallas_call(widen, out_shape=jax.ShapeDtypeStruct((cells, width), f32)...  2.15 us

profile of v3, /device:TPU:1, one launch (start us, length us, event | category | flops | bytes accessed | tf_op | source)
XLA Modules:
  0.0 72.3 jit_solution(6273658422386697190)
XLA Ops:
  0.0 70.2 %shard_map.91 = bf16[16,256,256]{2,1,0:T(8,128)(2,1)S(1)} custom-call(s32[2,4]{1,0:T(2,128)} %counts_hbm.1, s32[2,4096]{1,0:T(2,128)} %kin_hbm.1, f32[16,16,16]{2,1,0:T(8,128)} %relax_hbm.1, f32[4096,256]{1,0:T(8,128)} %bitcast.4, bf16[2048,768]{1,0:T(8,128)(2,1)} %a_hbm.1, bf16[2048,768]{1,0:T(8,128)(2,1)} %b_hbm.1, bf16[768,2048]{1,0:T(8,128)(2,1)} %c_hbm.1, ...), custom_call_target="tpu_custom_call" | custom-call | tf_op jit(solution)/shard_map/pallas_call | solution.py:498
  70.2 2.2 %shard_map.92 = f32[4096,256]{1,0:T(8,128)} custom-call(bf16[4096,256]{1,0:T(8,128)(2,1)S(1)} %bitcast.3), custom_call_target="tpu_custom_call" | custom-call | tf_op jit(solution)/shard_map/pallas_call | solution.py:541

commit v4 on v3

--- a/solution.py
+++ b/solution.py
@@ -61,9 +61,9 @@
 
 
 def kernel(dims, counts_hbm, kin_hbm, relax_hbm, dist, a_hbm, b_hbm, c_hbm, basis_hbm, back_hbm,
-           ret_out,
+           wide_out,
            cur, cprev, sendbuf, zsend, zrecv, recv, fown, fsend, halo, mv, outbuf,
-           map_a, map_b, map_c, basis, hid, coef, counts, kin_cells, relax,
+           map_a, map_b, map_c, basis, hid, coef, counts, kin_cells, relax, ret_out,
            load_sem, const_sem, local_sem, z_send, z_recv, row_send, row_recv, halo_send, halo_recv, res_send, res_recv):
     nx, ny, nz, width, groups, slabs = dims
     plane = ny * nz
@@ -107,20 +107,27 @@
 
     reach = 1 if ppd > 1 else 2
     barrier = pltpu.get_barrier_semaphore()
-    for p in range(1, groups):
-        pl.semaphore_signal(barrier, inc=1, device_id={"vel": lax.rem(me + p, groups)}, device_id_type=MESH)
     pl.semaphore_signal(barrier, inc=1, device_id={"space": ahead}, device_id_type=MESH)
     pl.semaphore_signal(barrier, inc=1, device_id={"space": behind}, device_id_type=MESH)
     for r in range(1, reach + 1):
         pl.semaphore_signal(barrier, inc=1, device_id=along(r), device_id_type=MESH)
         pl.semaphore_signal(barrier, inc=1, device_id=along(-r), device_id_type=MESH)
-
-    pieces = 4
+    for p in range(1, groups):
+        pl.semaphore_signal(barrier, inc=1, device_id={"vel": lax.rem(me + p, groups)}, device_id_type=MESH)
+
+    edge = 2 if ppd == 1 else 1
+    mid_count = groups - 2 * edge
+    far_count = groups - 4 * edge
+
+    def mid_dest(k):
+        return edge + lax.rem(mine + k, mid_count)
+
     loads = []
-    for n, c in enumerate((0, pieces - 1) + tuple(range(1, pieces - 1))):
-        size = cells // pieces
+    for n in range(groups):
+        size = ppd * plane
+        at = pl.multiple_of(lax.rem(mid_dest(0) - edge + n, groups) * size, size)
         loads.append(pltpu.make_async_copy(
-            dist.at[pl.ds(c * size, size)], cur.at[pl.ds(2 * plane + c * size, size)], load_sem.at[n]))
+            dist.at[pl.ds(at, size)], cur.at[pl.ds(2 * plane + at, size)], load_sem.at[n]))
         loads[-1].start()
     consts = []
     for n, (src, dst) in enumerate(((a_hbm, map_a), (b_hbm, map_b), (c_hbm, map_c.at[pl.ds(0, rank)]),
@@ -222,13 +229,6 @@
         @pl.when(r != 0)
         def _():
             row_copy(dest, peer, r, h).start()
-
-    edge = 2 if ppd == 1 else 1
-    mid_count = groups - 2 * edge
-    far_count = groups - 4 * edge
-
-    def mid_dest(k):
-        return edge + lax.rem(mine + k, mid_count)
 
     def edge_dest(k):
         n = lax.rem(mine + k, 2 * edge)
@@ -312,7 +312,7 @@
         def lhs():
             return rows[...].reshape(block_rows, nv)
 
-        @pl.loop(0, rank // TILE)
+        @pl.loop(0, rank // TILE, unroll=True)
         def _(n):
             cols = pl.ds(pl.multiple_of(n * TILE, TILE), TILE)
             first = jnp.dot(lhs(), map_a[:, cols], preferred_element_type=jnp.float32)
@@ -410,18 +410,22 @@
             outbuf.at[h, :, :, own_lanes(me)],
             ret_out.at[pl.ds(mine * ppd, ppd), pl.ds(h * half, half)], local_sem.at[1, h])
 
-    for copy in loads[:2]:
+    def widen(at, h):
+        here = (pl.ds(at * ppd, ppd), pl.ds(h * half, half))
+        wide_out[here] = ret_out[here].astype(jnp.float32)
+
+    for copy in loads[:2 * edge + 1]:
+        copy.wait()
+    transport(mid_dest(0), 0)
+    pl.semaphore_wait(barrier, groups + 1 + 2 * reach)
+    send(mid_dest(0), 0)
+    for copy in loads[2 * edge + 1:]:
         copy.wait()
     for n, at in enumerate((pick(nx, 2), pick(nx + 1, 3), pick(2, nx + 1))):
         zsend[n] = cur[pl.ds(pl.multiple_of(at * plane, plane), plane)].astype(jnp.bfloat16)
     z_list = [z_copies(h) for h in range(HALVES)]
-    for copy in loads[2:]:
-        copy.wait()
-    transport(mid_dest(0), 0)
-    pl.semaphore_wait(barrier, groups + 1 + 2 * reach)
     for copy in z_list[0] + z_list[1]:
         copy.start()
-    send(mid_dest(0), 0)
     for copy in consts:
         copy.start()
 
@@ -473,9 +477,11 @@
     for h in range(HALVES):
         for copy in z_list[h] + rows_in[h] + halos[h]:
             copy.wait_send()
-        for copy in results[h]:
+        res_local(h).wait()
+        widen(mine, h)
+        for r, copy in enumerate(results[h], 1):
             copy.wait()
-        res_local(h).wait()
+            widen(chain_of(slab, lax.rem(me - r + groups, groups)), h)
 
 
 def body(dist, relax_rate, kinetic_cells, kinetic_count, map_a, map_b, map_c):
@@ -497,7 +503,7 @@
     dma = pltpu.SemaphoreType.DMA
     ret = pl.pallas_call(
         functools.partial(kernel, dims),
-        out_shape=pltpu.VMEM((nx, plane, width), bf16),
+        out_shape=pltpu.VMEM((nx, plane, width), f32),
         in_specs=[any_space] * 9,
         out_specs=vmem,
         scratch_shapes=[
@@ -521,7 +527,8 @@
             pltpu.SMEM(kinetic_count.shape, jnp.int32),
             pltpu.VMEM(kinetic_cells.shape, jnp.int32),
             pltpu.VMEM(relax_rate.shape, f32),
-            dma((4,)),
+            pltpu.VMEM((nx, plane, width), bf16),
+            dma((groups,)),
             dma((8,)),
             dma((2, HALVES)),
             dma((HALVES, 2)),
@@ -534,33 +541,10 @@
             dma((HALVES, groups)),
         ],
         compiler_params=pltpu.CompilerParams(
-            collective_id=0, has_side_effects=True, vmem_limit_bytes=64880640),
+            collective_id=0, has_side_effects=True, vmem_limit_bytes=62783488),
     )(kinetic_count, kinetic_cells, relax_rate, dist.reshape(cells, width), map_a, map_b, map_c,
       jnp.asarray(basis), jnp.asarray(back))
-    parts = 16
-    out = pl.pallas_call(
-        widen,
-        out_shape=jax.ShapeDtypeStruct((cells, width), f32),
-        in_specs=[vmem],
-        out_specs=any_space,
-        scratch_shapes=[
-            pltpu.VMEM((parts, cells // parts, width), f32),
-            dma((parts,)),
-        ],
-        compiler_params=pltpu.CompilerParams(vmem_limit_bytes=16 << 20),
-    )(ret.reshape(cells, width))
-    return out.reshape(dist.shape)
-
-
-def widen(src, out, wide_buf, out_sem):
-    parts = out_sem.shape[0]
-    size = src.shape[0] // parts
-    outs = [pltpu.make_async_copy(wide_buf.at[n], out.at[pl.ds(n * size, size)], out_sem.at[n]) for n in range(parts)]
-    for n in range(parts):
-        wide_buf[n] = src[n * size:(n + 1) * size].astype(jnp.float32)
-        outs[n].start()
-    for copy in outs:
-        copy.wait()
+    return ret.reshape(dist.shape)
 
 
 def solution(mesh):

time: 72.5 us -> 72.5 us (level)
  local copies, waits for them, and re-layouts: 0 us -> 2.02 us
  Pallas kernels: 72.3 us -> 70.3 us
    pallas_call x1 -> x0, Pallas kernels: 2.15 us -> none  [body(): pl.pallas_call(widen, out_shape=jax.ShapeDtypeStruct((cells, width), f32)...]
    unnamed x0 -> x1, local copies, waits for them, and re-layouts: none -> 2.02 us
where the time goes in v4:
time: 72.5 us; the launch traced here: 72.4 us
  Pallas kernels  70.3 us (97%)
  local copies, waits for them, and re-layouts  2.02 us (3%)
    pallas_call x1, Pallas kernels, body(): pl.pallas_call(functools.partial(kernel, dims), out_shape=pltpu.VMEM((nx,...  70.3 us
    unnamed x1, local copies, waits for them, and re-layouts  2.02 us

profile of v4, /device:TPU:1, one launch (start us, length us, event | category | flops | bytes accessed | tf_op | source)
XLA Modules:
  0.0 72.4 jit_solution(807746398122668069)
XLA Ops:
  0.0 70.3 %shard_map.91 = f32[16,256,256]{2,1,0:T(8,128)S(1)} custom-call(s32[2,4]{1,0:T(2,128)} %counts_hbm.1, s32[2,4096]{1,0:T(2,128)} %kin_hbm.1, f32[16,16,16]{2,1,0:T(8,128)} %relax_hbm.1, f32[4096,256]{1,0:T(8,128)} %bitcast.3, bf16[2048,768]{1,0:T(8,128)(2,1)} %a_hbm.1, bf16[2048,768]{1,0:T(8,128)(2,1)} %b_hbm.1, bf16[768,2048]{1,0:T(8,128)(2,1)} %c_hbm.1, ...), custom_call_target="tpu_custom_call" | custom-call | tf_op jit(solution)/shard_map/pallas_call | solution.py:504
  70.3 2.0 %copy.11 = f32[16,16,16,256]{3,2,1,0:T(8,128)} copy(f32[16,16,16,256]{3,2,1,0:T(8,128)S(1)} %bitcast.2) | data formatting | bytes 8388608

commit v5 on v4

--- a/solution.py
+++ b/solution.py
@@ -120,7 +120,7 @@
     far_count = groups - 4 * edge
 
     def mid_dest(k):
-        return edge + lax.rem(mine + k, mid_count)
+        return edge + lax.rem(mine + k + 1, mid_count)
 
     loads = []
     for n in range(groups):

time: 72.5 us -> 72 us (level)
  no operation moved by 1% of the time
where the time goes in v5:
time: 72 us; the launch traced here: 71.8 us
  Pallas kernels  69.8 us (97%)
  local copies, waits for them, and re-layouts  2.02 us (3%)
    pallas_call x1, Pallas kernels, body(): pl.pallas_call(functools.partial(kernel, dims), out_shape=pltpu.VMEM((nx,...  69.8 us
    unnamed x1, local copies, waits for them, and re-layouts  2.02 us

profile of v5, /device:TPU:1, one launch (start us, length us, event | category | flops | bytes accessed | tf_op | source)
XLA Modules:
  0.0 71.8 jit_solution(5751010908382184020)
XLA Ops:
  0.0 69.8 %shard_map.91 = f32[16,256,256]{2,1,0:T(8,128)S(1)} custom-call(s32[2,4]{1,0:T(2,128)} %counts_hbm.1, s32[2,4096]{1,0:T(2,128)} %kin_hbm.1, f32[16,16,16]{2,1,0:T(8,128)} %relax_hbm.1, f32[4096,256]{1,0:T(8,128)} %bitcast.3, bf16[2048,768]{1,0:T(8,128)(2,1)} %a_hbm.1, bf16[2048,768]{1,0:T(8,128)(2,1)} %b_hbm.1, bf16[768,2048]{1,0:T(8,128)(2,1)} %c_hbm.1, ...), custom_call_target="tpu_custom_call" | custom-call | tf_op jit(solution)/shard_map/pallas_call | solution.py:504
  69.8 2.0 %copy.11 = f32[16,16,16,256]{3,2,1,0:T(8,128)} copy(f32[16,16,16,256]{3,2,1,0:T(8,128)S(1)} %bitcast.2) | data formatting | bytes 8388608
